TPU v7x, 32 devices: a whole 2x2x4 slice. The times are simulated.
32 devices in a mesh: grp: 2 (over y), tok: 4 (over z), sec: 2 (over core), ch: 2 (over x).
Axes of the slice: x: 2, y: 2, z: 4, core: 2. Of those that a mesh axis runs over, the one named last changes fastest.
Arguments:
- features: bfloat16 [4096, 2048], P('ch', ('grp', 'tok', 'sec')), parts along dimension 1, may hold values from -6 to 6
- gate_one: bfloat16 [4096, 2048], P('ch', ('grp', 'tok', 'sec')), parts along dimension 1, may hold values from -6 to 6
- taps_one: bfloat16 [4096, 128], P('ch'), may hold values from -0.5 to 0.5
- long_filter: bfloat16 [4096, 1024], P('ch', ('tok', 'sec')), may hold values from -0.1875 to 0.1875
- skip_gain: float32 [4096], P('ch'), may hold values from 0.5 to 1.5
- taps_two: bfloat16 [4096, 128], P('ch'), may hold values from -0.5 to 0.5
- gate_two: bfloat16 [4096, 2048], P('ch', ('grp', 'tok', 'sec')), parts along dimension 1, may hold values from -6 to 6
Outputs:
- mixed_out: bfloat16 [4096, 2048], P('ch', ('grp', 'tok', 'sec')), parts along dimension 1
There are 2 independent parts, one for each index of `grp`. A program takes and returns all parts, laid end to end along the dimension named above; an argument that names none is the same for every part. Nothing has to cross between parts.
All inputs are finite; a program needn't handle non-finite values.
Results may differ from a plain program's by a relative error of at most 0.0057.
Values may be sent and summed in bfloat16 or wider, within the bound.
No kernel may reach another device: no remote copies, remote signals or barrier semaphores. Data moves between devices by JAX's collectives and lax.ppermute only.
A program may use at most 192 MiB of HBM per device.

v0:
```python
import math
import jax
import jax.numpy as jnp
from jax import lax
from jax.sharding import PartitionSpec as P


def passed_along(array, axis, by):
    length = lax.axis_size(axis)
    pairs = [(i, i + by) for i in range(length) if 0 <= i + by < length]
    return lax.ppermute(array, axis, pairs)


def depthwise(padded, kernel_taps):
    tap_count = kernel_taps.shape[1]
    length = padded.shape[1] - (tap_count - 1)
    group_size = 16
    total = jnp.zeros((padded.shape[0], length), jnp.float32)
    for first in range(0, tap_count, group_size):
        last = min(first + group_size, tap_count)
        stacked = jnp.stack(
            [padded[:, tap_count - 1 - k : tap_count - 1 - k + length] for k in range(first, last)],
            axis=1,
        )
        total = total + jnp.einsum(
            "cgl,cg->cl", stacked, kernel_taps[:, first:last], preferred_element_type=jnp.float32
        )
    return total


def angle_table(rows_count, cols_count, period):
    row_index = jnp.arange(rows_count, dtype=jnp.int32)[:, None]
    col_index = jnp.arange(cols_count, dtype=jnp.int32)[None, :]
    phase = (row_index * col_index % period).astype(jnp.float32) * (2.0 * math.pi / period)
    return (jnp.cos(phase), jnp.sin(phase))


def contract(form, left, right):
    return jnp.einsum(form, left, right, precision=lax.Precision.HIGHEST)


def forward_spectrum(signal, outer, inner, total):
    half_outer = outer // 2
    cos_first, sin_first = angle_table(half_outer, outer, outer)
    turn_cos, turn_sin = angle_table(outer, inner, total)
    cos_inner, sin_inner = angle_table(inner, inner, inner)
    shaped = signal.reshape(signal.shape[0], half_outer, inner)
    real_a = contract("cmn,mk->ckn", shaped, cos_first)
    imag_a = -contract("cmn,mk->ckn", shaped, sin_first)
    real_b = real_a * turn_cos + imag_a * turn_sin
    imag_b = imag_a * turn_cos - real_a * turn_sin
    real_c = contract("ckn,nj->cjk", real_b, cos_inner) + contract("ckn,nj->cjk", imag_b, sin_inner)
    imag_c = contract("ckn,nj->cjk", imag_b, cos_inner) - contract("ckn,nj->cjk", real_b, sin_inner)
    return (real_c, imag_c)


def inverse_spectrum(real_y, imag_y, outer, inner, total):
    half_outer = outer // 2
    cos_inner, sin_inner = angle_table(inner, inner, inner)
    turn_cos, turn_sin = angle_table(outer, inner, total)
    cos_last, sin_last = angle_table(outer, half_outer, outer)
    real_c = contract("cjk,jn->ckn", real_y, cos_inner) - contract("cjk,jn->ckn", imag_y, sin_inner)
    imag_c = contract("cjk,jn->ckn", imag_y, cos_inner) + contract("cjk,jn->ckn", real_y, sin_inner)
    real_d = real_c * turn_cos - imag_c * turn_sin
    imag_d = imag_c * turn_cos + real_c * turn_sin
    result = contract("ckn,km->cmn", real_d, cos_last) - contract("ckn,km->cmn", imag_d, sin_last)
    return (result / total).reshape(real_y.shape[0], half_outer * inner)


def on_device(features, gate_one, taps_one, long_filter, skip_gain, taps_two, gate_two):
    shards = lax.axis_size(("tok", "sec"))
    channels, block_len = features.shape
    narrow = channels // shards
    seq_len = block_len * shards
    rim_width = taps_one.shape[1] - 1
    total = 2 * seq_len
    inner = math.gcd(seq_len, 128)
    outer = total // inner
    filter_rows = lax.all_to_all(
        long_filter[:, None, :], ("tok", "sec"), split_axis=0, concat_axis=1, tiled=True
    ).reshape(narrow, seq_len)
    rim_rows = passed_along(features[:, block_len - rim_width :], ("tok", "sec"), 1)
    first_conv = depthwise(jnp.concatenate([rim_rows, features], axis=1), taps_one)
    mixed_one = (first_conv * gate_one).astype(jnp.bfloat16)
    channel_rows = lax.all_to_all(
        mixed_one[:, None, :], ("tok", "sec"), split_axis=0, concat_axis=1, tiled=True
    )
    channel_rows = channel_rows.reshape(narrow, seq_len).astype(jnp.float32)
    filter_real, filter_imag = forward_spectrum(
        filter_rows.astype(jnp.float32), outer, inner, total
    )
    signal_real, signal_imag = forward_spectrum(channel_rows, outer, inner, total)
    product_real = signal_real * filter_real - signal_imag * filter_imag
    product_imag = signal_real * filter_imag + signal_imag * filter_real
    conv_rows = inverse_spectrum(product_real, product_imag, outer, inner, total)
    skip_local = lax.dynamic_slice_in_dim(
        skip_gain, lax.axis_index(("tok", "sec")) * narrow, narrow
    )
    long_out = (conv_rows + skip_local[:, None] * channel_rows).astype(jnp.bfloat16)
    long_blocks = long_out.reshape(narrow, shards, block_len)
    tail_rows = jnp.concatenate(
        [
            jnp.zeros((narrow, 1, rim_width), jnp.bfloat16),
            long_blocks[:, :-1, block_len - rim_width :],
        ],
        axis=1,
    )
    windows = jnp.concatenate([tail_rows, long_blocks], axis=2)
    padded = lax.all_to_all(
        windows, ("tok", "sec"), split_axis=1, concat_axis=0, tiled=True
    ).reshape(channels, block_len + rim_width)
    second_conv = depthwise(padded, taps_two)
    return (second_conv * gate_two).astype(jnp.bfloat16)


def solution(mesh):
    in_specs = (
        P("ch", ("grp", "tok", "sec")),
        P("ch", ("grp", "tok", "sec")),
        P("ch", None),
        P("ch", ("tok", "sec")),
        P("ch"),
        P("ch", None),
        P("ch", ("grp", "tok", "sec")),
    )
    out_specs = P("ch", ("grp", "tok", "sec"))
    return jax.shard_map(
        on_device, mesh=mesh, in_specs=in_specs, out_specs=out_specs, check_vma=False
    )
```

profile of v0, /device:TPU:0, one launch (start us, length us, event | category | flops | bytes accessed | tf_op | source)
XLA Modules:
  0.0 428.6 jit_solution(18028862349489927458)
XLA Ops:
  8.2 6.1 %all-to-all-start.1 = ((bf16[8,2,16384]{2,1,0:T(2,128)(2,1)}), bf16[8,2,16384]{2,1,0:T(2,128)(2,1)S(1)}, u32[]{:S(2)}, u32[]{:S(2)}) async-start(bf16[8,2,16384]{2,1,0:T(2,128)(2,1)} %reshape.112), calls=%async_computation.1 | async-start | bytes 1048576 | tf_op jit(solution)/shard_map/all_to_all | solution.py:79
  14.3 5.7 %slice_bitcast_fusion.142 = (bf16[2048,16,1]{1,0,2:T(8,128)(2,1)S(1)}, bf16[2048,16,1]{1,0,2:T(8,128)(2,1)}, bf16[2048,16,1]{1,0,2:T(8,128)(2,1)}, bf16[2048,16,...) fusion(bf16[2048,128]{1,0:T(8,128)(2,1)} %param.9), kind=kLoop, calls=%fused_computation.1013 | loop fusion | bytes 1048576 | tf_op jit(solution)/shard_map/slice | solution.py:26
  110.7 8.7 %fusion.16 = f32[2048,1,128]{2,1,0:T(1,128)S(1)} fusion(bf16[2048,16,128]{2,0,1:T(8,128)(2,1)} %constant_dynamic-update-slice_fusion.112, bf16[2048,16,1]{1,0,2:T(8,128)(2,1)S(1)} %get-tuple-element.191), kind=kOutput, calls=%fused_computation.268 | convolution fusion | flops 8388608 | bytes 9502720 | tf_op jit(solution)/shard_map/cgl,cg->cl/dot_general | solution.py:25
  119.4 8.7 %fusion.18 = f32[2048,1,128]{2,1,0:T(1,128)S(1)} fusion(bf16[2048,16,128]{2,0,1:T(8,128)(2,1)} %get-tuple-element.175, bf16[2048,16,1]{1,0,2:T(8,128)(2,1)S(1)} %get-tuple-element.192), kind=kOutput, calls=%fused_computation.270 | convolution fusion | flops 8388608 | bytes 9502720 | tf_op jit(solution)/shard_map/cgl,cg->cl/dot_general | solution.py:25
  128.2 9.0 %fusion.20 = f32[2048,1,128]{2,1,0:T(1,128)S(1)} fusion(bf16[2048,16,128]{2,0,1:T(8,128)(2,1)} %copy-done.9, bf16[2048,16,1]{1,0,2:T(8,128)(2,1)} %get-tuple-element.186), kind=kOutput, calls=%fused_computation.272 | convolution fusion | flops 8388608 | bytes 9502720 | tf_op jit(solution)/shard_map/cgl,cg->cl/dot_general | solution.py:25
  137.1 9.8 %fusion.22 = f32[2048,1,128]{2,1,0:T(1,128)} fusion(bf16[2048,16,128]{2,0,1:T(8,128)(2,1)} %copy-done.8, bf16[2048,16,1]{1,0,2:T(8,128)(2,1)} %get-tuple-element.187), kind=kOutput, calls=%fused_computation.274 | convolution fusion | flops 8388608 | bytes 9502720 | tf_op jit(solution)/shard_map/cgl,cg->cl/dot_general | solution.py:25
  146.9 10.2 %fusion.24 = f32[2048,1,128]{2,1,0:T(1,128)} fusion(bf16[2048,16,128]{2,0,1:T(8,128)(2,1)} %copy-done.7, bf16[2048,16,1]{1,0,2:T(8,128)(2,1)} %get-tuple-element.188), kind=kOutput, calls=%fused_computation.276 | convolution fusion | flops 8388608 | bytes 9502720 | tf_op jit(solution)/shard_map/cgl,cg->cl/dot_general | solution.py:25
  157.1 9.8 %fusion.26 = f32[2048,1,128]{2,1,0:T(1,128)} fusion(bf16[2048,16,128]{2,0,1:T(8,128)(2,1)} %copy-done.6, bf16[2048,16,1]{1,0,2:T(8,128)(2,1)} %get-tuple-element.189), kind=kOutput, calls=%fused_computation.278 | convolution fusion | flops 8388608 | bytes 9502720 | tf_op jit(solution)/shard_map/cgl,cg->cl/dot_general | solution.py:25
  166.8 9.9 %fusion.30 = f32[2048,1,128]{2,1,0:T(1,128)} fusion(bf16[2048,16,128]{2,0,1:T(8,128)(2,1)} %get-tuple-element.149, bf16[2048,16,1]{1,0,2:T(8,128)(2,1)S(1)} %get-tuple-element.190), kind=kOutput, calls=%fused_computation.282 | convolution fusion | flops 8388608 | bytes 9502720 | tf_op jit(solution)/shard_map/cgl,cg->cl/dot_general | solution.py:25
  176.7 9.8 %fusion.28 = f32[2048,1,128]{2,1,0:T(1,128)} fusion(bf16[2048,16,128]{2,0,1:T(8,128)(2,1)} %get-tuple-element.141, bf16[2048,16,1]{1,0,2:T(8,128)(2,1)S(1)} %get-tuple-element.185), kind=kOutput, calls=%fused_computation.280 | convolution fusion | flops 8388608 | bytes 9502720 | tf_op jit(solution)/shard_map/cgl,cg->cl/dot_general | solution.py:25
  191.4 5.1 %all-to-all-start = ((bf16[8,2,16384]{2,1,0:T(2,128)(2,1)}), bf16[8,2,16384]{2,1,0:T(2,128)(2,1)}, u32[]{:S(2)}, u32[]{:S(2)}) async-start(bf16[8,2,16384]{2,1,0:T(2,128)(2,1)} %reshape.110), calls=%async_computation | async-start | bytes 1048576 | tf_op jit(solution)/shard_map/all_to_all | solution.py:85
  201.5 10.4 %all-to-all-done = bf16[8,2,16384]{2,1,0:T(2,128)(2,1)} async-done(((bf16[8,2,16384]{2,1,0:T(2,128)(2,1)}), bf16[8,2,16384]{2,1,0:T(2,128)(2,1)}, u32[]{:S(2)}, u32[]{:S(2)}) %all-to-all-start) | async-done | bytes 524320 | tf_op jit(solution)/shard_map/all_to_all | solution.py:85
  248.6 4.0 fusion.73
  252.5 3.8 multiply_subtract_fusion
  263.2 3.7 all-to-all-start.2
  269.6 23.6 %all-to-all-done.2 = bf16[256,8,255]{2,0,1:T(8,128)(2,1)S(1)} async-done(((bf16[256,8,255]{2,0,1:T(8,128)(2,1)}), bf16[256,8,255]{2,0,1:T(8,128)(2,1)S(1)}, u32[]{:S(2)}, u32[]{:S(2)}) %all-to-all-start.2) | async-done | bytes 1044512 | tf_op jit(solution)/shard_map/all_to_all | solution.py:109
  349.6 9.1 %fusion.14 = f32[2048,1,128]{2,1,0:T(1,128)S(1)} fusion(bf16[2048,16,128]{2,0,1:T(8,128)(2,1)} %get-tuple-element.20, bf16[2048,16,1]{1,0,2:T(8,128)(2,1)S(1)} %copy-done.5), kind=kOutput, calls=%fused_computation.266 | convolution fusion | flops 8388608 | bytes 9502720 | tf_op jit(solution)/shard_map/cgl,cg->cl/dot_general | solution.py:25
  358.7 8.7 %fusion.12 = f32[2048,1,128]{2,1,0:T(1,128)S(1)} fusion(bf16[2048,16,128]{2,0,1:T(8,128)(2,1)} %copy-done.10, bf16[2048,16,1]{1,0,2:T(8,128)(2,1)S(1)} %copy-done.4), kind=kOutput, calls=%fused_computation.264 | convolution fusion | flops 8388608 | bytes 9502720 | tf_op jit(solution)/shard_map/cgl,cg->cl/dot_general | solution.py:25
  367.5 8.9 %fusion.10 = f32[2048,1,128]{2,1,0:T(1,128)S(1)} fusion(bf16[2048,16,128]{2,0,1:T(8,128)(2,1)} %get-tuple-element.19, bf16[2048,16,1]{1,0,2:T(8,128)(2,1)S(1)} %get-tuple-element.181), kind=kOutput, calls=%fused_computation.262 | convolution fusion | flops 8388608 | bytes 9502720 | tf_op jit(solution)/shard_map/cgl,cg->cl/dot_general | solution.py:25
  376.4 8.8 %fusion.8 = f32[2048,1,128]{2,1,0:T(1,128)S(1)} fusion(bf16[2048,16,128]{2,0,1:T(8,128)(2,1)} %get-tuple-element.18, bf16[2048,16,1]{1,0,2:T(8,128)(2,1)} %get-tuple-element.180), kind=kOutput, calls=%fused_computation.260 | convolution fusion | flops 8388608 | bytes 9502720 | tf_op jit(solution)/shard_map/cgl,cg->cl/dot_general | solution.py:25
  385.1 9.9 %fusion.6 = f32[2048,1,128]{2,1,0:T(1,128)} fusion(bf16[2048,16,128]{2,0,1:T(8,128)(2,1)} %get-tuple-element.17, bf16[2048,16,1]{1,0,2:T(8,128)(2,1)} %get-tuple-element.179), kind=kOutput, calls=%fused_computation.258 | convolution fusion | flops 8388608 | bytes 9502720 | tf_op jit(solution)/shard_map/cgl,cg->cl/dot_general | solution.py:25
  395.0 9.8 %fusion.4 = f32[2048,1,128]{2,1,0:T(1,128)} fusion(bf16[2048,16,128]{2,0,1:T(8,128)(2,1)} %get-tuple-element.16, bf16[2048,16,1]{1,0,2:T(8,128)(2,1)} %get-tuple-element.178), kind=kOutput, calls=%fused_computation.256 | convolution fusion | flops 8388608 | bytes 9502720 | tf_op jit(solution)/shard_map/cgl,cg->cl/dot_general | solution.py:25
  404.8 9.7 %fusion.2 = f32[2048,1,128]{2,1,0:T(1,128)} fusion(bf16[2048,16,128]{2,0,1:T(8,128)(2,1)} %copy-done.12, bf16[2048,16,1]{1,0,2:T(8,128)(2,1)S(1)} %get-tuple-element.184), kind=kOutput, calls=%fused_computation.254 | convolution fusion | flops 8388608 | bytes 9502720 | tf_op jit(solution)/shard_map/cgl,cg->cl/dot_general | solution.py:25
  414.5 10.1 %fusion = f32[2048,1,128]{2,1,0:T(1,128)} fusion(bf16[2048,16,128]{2,0,1:T(8,128)(2,1)} %copy-done.11, bf16[2048,16,1]{1,0,2:T(8,128)(2,1)} %get-tuple-element.183), kind=kOutput, calls=%fused_computation.252 | convolution fusion | flops 8388608 | bytes 9502720 | tf_op jit(solution)/shard_map/cgl,cg->cl/dot_general | solution.py:25
  (180 shorter events, 214.6 us)
Async XLA Ops:
  0.0 20.0 %copy-start = (bf16[2048,128]{1,0:T(8,128)(2,1)S(1)}, bf16[2048,128]{1,0:T(8,128)(2,1)}, u32[]{:S(2)}) copy-start(bf16[2048,128]{1,0:T(8,128)(2,1)} %param.7) | copy-start | bytes 1572868
  2.1 17.9 %collective-permute-start = (bf16[2048,127]{1,0:T(8,128)(2,1)}, bf16[2048,127]{1,0:T(8,128)(2,1)S(1)}, u32[]{:S(2)}, u32[]{:S(2)}) collective-permute-start(bf16[2048,127]{1,0:T(8,128)(2,1)} %slice.819), channel_id=1, source_target_pairs={{0,2},{2,4},{4,6},{6,8},{8,10},{10,12},{12,14},{1,3},{3,5},{5,7},{... | collective-permute-start | bytes 1560584 | tf_op jit(solution)/shard_map/ppermute | solution.py:11
  8.2 183.2 %all-to-all-start.1 = ((bf16[8,2,16384]{2,1,0:T(2,128)(2,1)}), bf16[8,2,16384]{2,1,0:T(2,128)(2,1)S(1)}, u32[]{:S(2)}, u32[]{:S(2)}) async-start(bf16[8,2,16384]{2,1,0:T(2,128)(2,1)} %reshape.112), calls=%async_computation.1 | async-start | bytes 1048576 | tf_op jit(solution)/shard_map/all_to_all | solution.py:79
  28.0 3.2 copy-start.13
  63.3 5.3 %copy-start.6 = (bf16[2048,16,128]{2,0,1:T(8,128)(2,1)}, bf16[2048,16,128]{2,0,1:T(8,128)(2,1)S(1)}, u32[]{:S(2)}) copy-start(bf16[2048,16,128]{2,0,1:T(8,128)(2,1)S(1)} %get-tuple-element.157) | copy-start | bytes 25165828
  71.9 5.3 %copy-start.7 = (bf16[2048,16,128]{2,0,1:T(8,128)(2,1)}, bf16[2048,16,128]{2,0,1:T(8,128)(2,1)S(1)}, u32[]{:S(2)}) copy-start(bf16[2048,16,128]{2,0,1:T(8,128)(2,1)S(1)} %get-tuple-element.163) | copy-start | bytes 25165828
  79.6 7.1 %copy-start.8 = (bf16[2048,16,128]{2,0,1:T(8,128)(2,1)}, bf16[2048,16,128]{2,0,1:T(8,128)(2,1)S(1)}, u32[]{:S(2)}) copy-start(bf16[2048,16,128]{2,0,1:T(8,128)(2,1)S(1)} %get-tuple-element.168) | copy-start | bytes 25165828
  86.7 14.3 %copy-start.9 = (bf16[2048,16,128]{2,0,1:T(8,128)(2,1)}, bf16[2048,16,128]{2,0,1:T(8,128)(2,1)S(1)}, u32[]{:S(2)}) copy-start(bf16[2048,16,128]{2,0,1:T(8,128)(2,1)S(1)} %get-tuple-element.172) | copy-start | bytes 25165828
  176.7 9.8 %copy-start.2 = (bf16[2048,128]{1,0:T(8,128)(2,1)S(1)}, bf16[2048,128]{1,0:T(8,128)(2,1)}, u32[]{:S(2)}) copy-start(bf16[2048,128]{1,0:T(8,128)(2,1)} %param.8) | copy-start | bytes 1572868
  191.4 20.5 %all-to-all-start = ((bf16[8,2,16384]{2,1,0:T(2,128)(2,1)}), bf16[8,2,16384]{2,1,0:T(2,128)(2,1)}, u32[]{:S(2)}, u32[]{:S(2)}) async-start(bf16[8,2,16384]{2,1,0:T(2,128)(2,1)} %reshape.110), calls=%async_computation | async-start | bytes 1048576 | tf_op jit(solution)/shard_map/all_to_all | solution.py:85
  256.3 10.6 %copy-start.1 = (bf16[2048,128]{1,0:T(8,128)(2,1)S(1)}, bf16[2048,128]{1,0:T(8,128)(2,1)}, u32[]{:S(2)}) copy-start(bf16[2048,128]{1,0:T(8,128)(2,1)} %param.12) | copy-start | bytes 1572868
  263.2 30.1 %all-to-all-start.2 = ((bf16[256,8,255]{2,0,1:T(8,128)(2,1)}), bf16[256,8,255]{2,0,1:T(8,128)(2,1)S(1)}, u32[]{:S(2)}, u32[]{:S(2)}) async-start(bf16[256,8,255]{2,0,1:T(8,128)(2,1)} %copy.106), calls=%async_computation.2 | async-start | bytes 2097152 | tf_op jit(solution)/shard_map/all_to_all | solution.py:109
  335.5 14.1 %copy-start.5 = (bf16[2048,16,1]{1,0,2:T(8,128)(2,1)S(1)}, bf16[2048,16,1]{1,0,2:T(8,128)(2,1)}, u32[]{:S(2)}) copy-start(bf16[2048,16,1]{1,0,2:T(8,128)(2,1)} %get-tuple-element.182) | copy-start | bytes 196612
  341.4 3.2 copy-start.10
  341.4 5.8 %copy-start.11 = (bf16[2048,16,128]{2,0,1:T(8,128)(2,1)}, bf16[2048,16,128]{2,0,1:T(8,128)(2,1)S(1)}, u32[]{:S(2)}) copy-start(bf16[2048,16,128]{2,0,1:T(8,128)(2,1)S(1)} %get-tuple-element.14) | copy-start | bytes 25165828
  341.4 8.2 %copy-start.12 = (bf16[2048,16,128]{2,0,1:T(8,128)(2,1)}, bf16[2048,16,128]{2,0,1:T(8,128)(2,1)S(1)}, u32[]{:S(2)}) copy-start(bf16[2048,16,128]{2,0,1:T(8,128)(2,1)S(1)} %get-tuple-element.15) | copy-start | bytes 25165828
  341.4 17.4 %copy-start.4 = (bf16[2048,16,1]{1,0,2:T(8,128)(2,1)S(1)}, bf16[2048,16,1]{1,0,2:T(8,128)(2,1)}, u32[]{:S(2)}) copy-start(bf16[2048,16,1]{1,0,2:T(8,128)(2,1)} %get-tuple-element.177) | copy-start | bytes 196612
  414.5 10.1 %copy-start.3 = (bf16[2048,128]{1,0:T(8,128)(2,1)S(1)}, bf16[2048,128]{1,0:T(8,128)(2,1)}, u32[]{:S(2)}) copy-start(bf16[2048,128]{1,0:T(8,128)(2,1)} %param.13) | copy-start | bytes 1572868
where the time goes:
time: 436 us; the launch traced here: 429 us
  matrix products  201 us (46%)
  other arithmetic  97.6 us (22%)
  local copies, waits for them, and re-layouts  78 us (18%)
  waiting for transfers between devices  34.1 us (8%)
  starting transfers between devices  17.4 us (4%)
    dot_general x16, matrix products, depthwise(): jnp.einsum('cgl,cg->cl', stacked, kernel_taps[:, first:last], preferred_e...  151 us
    unnamed x91, other arithmetic  67.5 us
    unnamed x49, local copies, waits for them, and re-layouts  62 us
    dot_general x18, matrix products, contract(): return jnp.einsum(form, left, right, precision=lax.Precision.HIGHEST)  50 us
    all_to_all x1, waiting for transfers between devices, on_device(): lax.all_to_all(windows, ('tok', 'sec'), split_axis=1, concat_axis=0, tile...  23.6 us
    another operation x8, other arithmetic, depthwise(): jnp.stack([padded[:, tap_count - 1 - k:tap_count - 1 - k + length] for k...  19.8 us
    all_to_all x1, waiting for transfers between devices, on_device(): lax.all_to_all(mixed_one[:, None, :], ('tok', 'sec'), split_axis=0, conca...  10.4 us
  transfers between devices with their start and end apart: 4, of which 2 were waited for; matrix products, arithmetic and copies ran while one was open for 43% of the time, Pallas kernels for 0%

commit v1 on v0

--- a/solution.py
+++ b/solution.py
@@ -3,6 +3,29 @@
 import jax.numpy as jnp
 from jax import lax
 from jax.sharding import PartitionSpec as P
+
+
+def cut_along(x, dim, size):
+    shape = x.shape
+    blocks = x.reshape(*shape[:dim], size, shape[dim] // size, *shape[dim + 1 :])
+    return jnp.moveaxis(blocks, dim, 0)
+
+
+def in_order(blocks, dim):
+    lengths = list(blocks.shape[1:])
+    lengths[dim] *= blocks.shape[0]
+    return jnp.moveaxis(blocks, 0, dim).reshape(lengths)
+
+
+def exchange_directly(x, axis, split_dim, concat_dim):
+    size, here = (lax.axis_size(axis), lax.axis_index(axis))
+    pieces = cut_along(x, split_dim, size)
+    outs = [pieces[here]]
+    for turn in range(1, size):
+        sent = pieces[(here + turn) % size]
+        outs.append(lax.ppermute(sent, axis, [(i, (i + turn) % size) for i in range(size)]))
+    pieces = jnp.stack(outs)[(here - jnp.arange(size)) % size]
+    return in_order(pieces, concat_dim)
 
 
 def passed_along(array, axis, by):
@@ -106,9 +129,9 @@
         axis=1,
     )
     windows = jnp.concatenate([tail_rows, long_blocks], axis=2)
-    padded = lax.all_to_all(
-        windows, ("tok", "sec"), split_axis=1, concat_axis=0, tiled=True
-    ).reshape(channels, block_len + rim_width)
+    padded = exchange_directly(windows, ("tok", "sec"), 1, 0).reshape(
+        channels, block_len + rim_width
+    )
     second_conv = depthwise(padded, taps_two)
     return (second_conv * gate_two).astype(jnp.bfloat16)
 

time: 436 us -> 459 us (1.053)
  the two profiles are of different devices: /device:TPU:0 before, /device:TPU:15 now
where the time goes in v1:
time: 459 us; the launch traced here: 451 us
  matrix products  201 us (44%)
  other arithmetic  97 us (21%)
  local copies, waits for them, and re-layouts  80.4 us (18%)
  waiting for transfers between devices  48.5 us (11%)
  starting transfers between devices  23.4 us (5%)
    dot_general x16, matrix products, depthwise(): jnp.einsum('cgl,cg->cl', stacked, kernel_taps[:, first:last], preferred_e...  151 us
    unnamed x91, other arithmetic  67.1 us
    unnamed x74, local copies, waits for them, and re-layouts  61.7 us
    dot_general x18, matrix products, contract(): return jnp.einsum(form, left, right, precision=lax.Precision.HIGHEST)  50 us
    ppermute x7, waiting for transfers between devices, exchange_directly(): lax.ppermute(sent, axis, [(i, (i + turn) % size) for i in range(size)])  41 us
    another operation x8, other arithmetic, depthwise(): jnp.stack([padded[:, tap_count - 1 - k:tap_count - 1 - k + length] for k...  19.7 us
    ppermute x7, starting transfers between devices, exchange_directly(): lax.ppermute(sent, axis, [(i, (i + turn) % size) for i in range(size)])  10.5 us
  transfers between devices with their start and end apart: 10, of which 6 were waited for; matrix products, arithmetic and copies ran while one was open for 41% of the time, Pallas kernels for 0%

profile of v1, /device:TPU:15, one launch (start us, length us, event | category | flops | bytes accessed | tf_op | source)
XLA Modules:
  0.0 451.3 jit_solution(11562362181308214435)
XLA Ops:
  2.1 3.8 collective-permute-start
  9.4 4.0 all-to-all-start.1
  13.4 5.7 %slice_bitcast_fusion.142 = (bf16[2048,16,1]{1,0,2:T(8,128)(2,1)}, bf16[2048,16,1]{1,0,2:T(8,128)(2,1)}, bf16[2048,16,1]{1,0,2:T(8,128)(2,1)}, bf16[2048,16,1]{1...) fusion(bf16[2048,128]{1,0:T(8,128)(2,1)} %param.9), kind=kLoop, calls=%fused_computation.1022 | loop fusion | bytes 1048576 | tf_op jit(solution)/shard_map/slice | solution.py:49
  113.1 8.7 %fusion.16 = f32[2048,1,128]{2,1,0:T(1,128)S(1)} fusion(bf16[2048,16,128]{2,0,1:T(8,128)(2,1)} %constant_dynamic-update-slice_fusion.112, bf16[2048,16,1]{1,0,2:T(8,128)(2,1)S(1)} %get-tuple-element.199), kind=kOutput, calls=%fused_computation.269 | convolution fusion | flops 8388608 | bytes 9502720 | tf_op jit(solution)/shard_map/cgl,cg->cl/dot_general | solution.py:48
  121.8 8.8 %fusion.18 = f32[2048,1,128]{2,1,0:T(1,128)S(1)} fusion(bf16[2048,16,128]{2,0,1:T(8,128)(2,1)} %get-tuple-element.183, bf16[2048,16,1]{1,0,2:T(8,128)(2,1)S(1)} %get-tuple-element.200), kind=kOutput, calls=%fused_computation.271 | convolution fusion | flops 8388608 | bytes 9502720 | tf_op jit(solution)/shard_map/cgl,cg->cl/dot_general | solution.py:48
  130.6 9.2 %fusion.20 = f32[2048,1,128]{2,1,0:T(1,128)S(1)} fusion(bf16[2048,16,128]{2,0,1:T(8,128)(2,1)} %copy-done.18, bf16[2048,16,1]{1,0,2:T(8,128)(2,1)S(1)} %copy-done.14), kind=kOutput, calls=%fused_computation.273 | convolution fusion | flops 8388608 | bytes 9502720 | tf_op jit(solution)/shard_map/cgl,cg->cl/dot_general | solution.py:48
  139.8 9.8 %fusion.22 = f32[2048,1,128]{2,1,0:T(1,128)} fusion(bf16[2048,16,128]{2,0,1:T(8,128)(2,1)} %copy-done.17, bf16[2048,16,1]{1,0,2:T(8,128)(2,1)S(1)} %copy-done.13), kind=kOutput, calls=%fused_computation.275 | convolution fusion | flops 8388608 | bytes 9502720 | tf_op jit(solution)/shard_map/cgl,cg->cl/dot_general | solution.py:48
  149.6 10.0 %fusion.24 = f32[2048,1,128]{2,1,0:T(1,128)} fusion(bf16[2048,16,128]{2,0,1:T(8,128)(2,1)} %copy-done.16, bf16[2048,16,1]{1,0,2:T(8,128)(2,1)S(1)} %copy-done.12), kind=kOutput, calls=%fused_computation.277 | convolution fusion | flops 8388608 | bytes 9502720 | tf_op jit(solution)/shard_map/cgl,cg->cl/dot_general | solution.py:48
  159.5 9.8 %fusion.26 = f32[2048,1,128]{2,1,0:T(1,128)} fusion(bf16[2048,16,128]{2,0,1:T(8,128)(2,1)} %copy-done.15, bf16[2048,16,1]{1,0,2:T(8,128)(2,1)S(1)} %copy-done.11), kind=kOutput, calls=%fused_computation.279 | convolution fusion | flops 8388608 | bytes 9502720 | tf_op jit(solution)/shard_map/cgl,cg->cl/dot_general | solution.py:48
  169.3 10.2 %fusion.30 = f32[2048,1,128]{2,1,0:T(1,128)} fusion(bf16[2048,16,128]{2,0,1:T(8,128)(2,1)} %get-tuple-element.157, bf16[2048,16,1]{1,0,2:T(8,128)(2,1)S(1)} %copy-done.10), kind=kOutput, calls=%fused_computation.283 | convolution fusion | flops 8388608 | bytes 9502720 | tf_op jit(solution)/shard_map/cgl,cg->cl/dot_general | solution.py:48
  179.5 9.8 %fusion.28 = f32[2048,1,128]{2,1,0:T(1,128)} fusion(bf16[2048,16,128]{2,0,1:T(8,128)(2,1)} %get-tuple-element.149, bf16[2048,16,1]{1,0,2:T(8,128)(2,1)S(1)} %copy-done.9), kind=kOutput, calls=%fused_computation.281 | convolution fusion | flops 8388608 | bytes 9502720 | tf_op jit(solution)/shard_map/cgl,cg->cl/dot_general | solution.py:48
  194.2 5.1 %all-to-all-start = ((bf16[8,2,16384]{2,1,0:T(2,128)(2,1)}), bf16[8,2,16384]{2,1,0:T(2,128)(2,1)}, u32[]{:S(2)}, u32[]{:S(2)}) async-start(bf16[8,2,16384]{2,1,0:T(2,128)(2,1)} %reshape.197), calls=%async_computation | async-start | bytes 1048576 | tf_op jit(solution)/shard_map/all_to_all | solution.py:108
  203.6 7.5 %all-to-all-done = bf16[8,2,16384]{2,1,0:T(2,128)(2,1)} async-done(((bf16[8,2,16384]{2,1,0:T(2,128)(2,1)}), bf16[8,2,16384]{2,1,0:T(2,128)(2,1)}, u32[]{:S(2)}, u32[]{:S(2)}) %all-to-all-start) | async-done | bytes 524320 | tf_op jit(solution)/shard_map/all_to_all | solution.py:108
  277.9 26.8 %collective-permute-done.3 = bf16[256,1,255]{2,1,0:T(2,128)(2,1)S(1)} collective-permute-done((bf16[256,1,255]{2,1,0:T(2,128)(2,1)S(1)}, bf16[256,1,255]{2,1,0:T(2,128)(2,1)S(1)}, u32[]{:S(2)}, u32[]{:S(2)}) %collective-permute-start.3) | collective-permute-done | bytes 130592 | tf_op jit(solution)/shard_map/ppermute | solution.py:26
  304.7 5.6 %collective-permute-done.4 = bf16[256,1,255]{2,1,0:T(2,128)(2,1)S(1)} collective-permute-done((bf16[256,1,255]{2,1,0:T(2,128)(2,1)S(1)}, bf16[256,1,255]{2,1,0:T(2,128)(2,1)S(1)}, u32[]{:S(2)}, u32[]{:S(2)}) %collective-permute-start.4) | collective-permute-done | bytes 130592 | tf_op jit(solution)/shard_map/ppermute | solution.py:26
  310.4 5.0 %collective-permute-done.6 = bf16[256,1,255]{2,1,0:T(2,128)(2,1)S(1)} collective-permute-done((bf16[256,1,255]{2,1,0:T(2,128)(2,1)S(1)}, bf16[256,1,255]{2,1,0:T(2,128)(2,1)S(1)}, u32[]{:S(2)}, u32[]{:S(2)}) %collective-permute-start.6) | collective-permute-done | bytes 130592 | tf_op jit(solution)/shard_map/ppermute | solution.py:26
  372.3 8.9 %fusion.14 = f32[2048,1,128]{2,1,0:T(1,128)S(1)} fusion(bf16[2048,16,128]{2,0,1:T(8,128)(2,1)} %get-tuple-element.20, bf16[2048,16,1]{1,0,2:T(8,128)(2,1)S(1)} %copy-done.8), kind=kOutput, calls=%fused_computation.267 | convolution fusion | flops 8388608 | bytes 9502720 | tf_op jit(solution)/shard_map/cgl,cg->cl/dot_general | solution.py:48
  381.3 8.8 %fusion.12 = f32[2048,1,128]{2,1,0:T(1,128)S(1)} fusion(bf16[2048,16,128]{2,0,1:T(8,128)(2,1)} %copy-done.19, bf16[2048,16,1]{1,0,2:T(8,128)(2,1)S(1)} %copy-done.7), kind=kOutput, calls=%fused_computation.265 | convolution fusion | flops 8388608 | bytes 9502720 | tf_op jit(solution)/shard_map/cgl,cg->cl/dot_general | solution.py:48
  390.0 9.1 %fusion.10 = f32[2048,1,128]{2,1,0:T(1,128)S(1)} fusion(bf16[2048,16,128]{2,0,1:T(8,128)(2,1)} %get-tuple-element.19, bf16[2048,16,1]{1,0,2:T(8,128)(2,1)S(1)} %copy-done.6), kind=kOutput, calls=%fused_computation.263 | convolution fusion | flops 8388608 | bytes 9502720 | tf_op jit(solution)/shard_map/cgl,cg->cl/dot_general | solution.py:48
  399.2 8.8 %fusion.8 = f32[2048,1,128]{2,1,0:T(1,128)S(1)} fusion(bf16[2048,16,128]{2,0,1:T(8,128)(2,1)} %get-tuple-element.18, bf16[2048,16,1]{1,0,2:T(8,128)(2,1)} %get-tuple-element.188), kind=kOutput, calls=%fused_computation.261 | convolution fusion | flops 8388608 | bytes 9502720 | tf_op jit(solution)/shard_map/cgl,cg->cl/dot_general | solution.py:48
  408.0 9.7 %fusion.6 = f32[2048,1,128]{2,1,0:T(1,128)} fusion(bf16[2048,16,128]{2,0,1:T(8,128)(2,1)} %get-tuple-element.17, bf16[2048,16,1]{1,0,2:T(8,128)(2,1)S(1)} %copy-done.5), kind=kOutput, calls=%fused_computation.259 | convolution fusion | flops 8388608 | bytes 9502720 | tf_op jit(solution)/shard_map/cgl,cg->cl/dot_general | solution.py:48
  417.7 10.0 %fusion.4 = f32[2048,1,128]{2,1,0:T(1,128)} fusion(bf16[2048,16,128]{2,0,1:T(8,128)(2,1)} %get-tuple-element.16, bf16[2048,16,1]{1,0,2:T(8,128)(2,1)} %get-tuple-element.186), kind=kOutput, calls=%fused_computation.257 | convolution fusion | flops 8388608 | bytes 9502720 | tf_op jit(solution)/shard_map/cgl,cg->cl/dot_general | solution.py:48
  427.7 9.7 %fusion.2 = f32[2048,1,128]{2,1,0:T(1,128)} fusion(bf16[2048,16,128]{2,0,1:T(8,128)(2,1)} %copy-done.21, bf16[2048,16,1]{1,0,2:T(8,128)(2,1)S(1)} %copy-done.4), kind=kOutput, calls=%fused_computation.255 | convolution fusion | flops 8388608 | bytes 9502720 | tf_op jit(solution)/shard_map/cgl,cg->cl/dot_general | solution.py:48
  437.4 10.0 %fusion = f32[2048,1,128]{2,1,0:T(1,128)} fusion(bf16[2048,16,128]{2,0,1:T(8,128)(2,1)} %copy-done.20, bf16[2048,16,1]{1,0,2:T(8,128)(2,1)} %get-tuple-element.191), kind=kOutput, calls=%fused_computation.253 | convolution fusion | flops 8388608 | bytes 9502720 | tf_op jit(solution)/shard_map/cgl,cg->cl/dot_general | solution.py:48
  (221 shorter events, 235.7 us)
Async XLA Ops:
  0.0 19.9 %copy-start.1 = (bf16[2048,128]{1,0:T(8,128)(2,1)S(1)}, bf16[2048,128]{1,0:T(8,128)(2,1)}, u32[]{:S(2)}) copy-start(bf16[2048,128]{1,0:T(8,128)(2,1)} %param.12) | copy-start | bytes 1572868
  2.1 20.8 %collective-permute-start = (bf16[2048,127]{1,0:T(8,128)(2,1)}, bf16[2048,127]{1,0:T(8,128)(2,1)S(1)}, u32[]{:S(2)}, u32[]{:S(2)}) collective-permute-start(bf16[2048,127]{1,0:T(8,128)(2,1)} %slice.819), channel_id=1, source_target_pairs={{0,2},{2,4},{4,6},{6,8},{8,10},{10,12},{12,14},{1,3},{3,5},{5,7},{... | collective-permute-start | bytes 1560584 | tf_op jit(solution)/shard_map/ppermute | solution.py:34
  9.4 184.8 %all-to-all-start.1 = ((bf16[8,2,16384]{2,1,0:T(2,128)(2,1)}), bf16[8,2,16384]{2,1,0:T(2,128)(2,1)S(1)}, u32[]{:S(2)}, u32[]{:S(2)}) async-start(bf16[8,2,16384]{2,1,0:T(2,128)(2,1)} %reshape.199), calls=%async_computation.1 | async-start | bytes 1048576 | tf_op jit(solution)/shard_map/all_to_all | solution.py:102
  13.4 9.5 %copy-start = (bf16[2048,128]{1,0:T(8,128)(2,1)S(1)}, bf16[2048,128]{1,0:T(8,128)(2,1)}, u32[]{:S(2)}) copy-start(bf16[2048,128]{1,0:T(8,128)(2,1)} %param.7) | copy-start | bytes 1572868
  89.3 14.2 %copy-start.18 = (bf16[2048,16,128]{2,0,1:T(8,128)(2,1)}, bf16[2048,16,128]{2,0,1:T(8,128)(2,1)S(1)}, u32[]{:S(2)}) copy-start(bf16[2048,16,128]{2,0,1:T(8,128)(2,1)S(1)} %get-tuple-element.180) | copy-start | bytes 25165828
  130.6 9.2 %copy-start.13 = (bf16[2048,16,1]{1,0,2:T(8,128)(2,1)S(1)}, bf16[2048,16,1]{1,0,2:T(8,128)(2,1)}, u32[]{:S(2)}) copy-start(bf16[2048,16,1]{1,0,2:T(8,128)(2,1)} %get-tuple-element.195) | copy-start | bytes 196612
  139.8 9.8 %copy-start.12 = (bf16[2048,16,1]{1,0,2:T(8,128)(2,1)S(1)}, bf16[2048,16,1]{1,0,2:T(8,128)(2,1)}, u32[]{:S(2)}) copy-start(bf16[2048,16,1]{1,0,2:T(8,128)(2,1)} %get-tuple-element.196) | copy-start | bytes 196612
  149.5 10.0 %copy-start.11 = (bf16[2048,16,1]{1,0,2:T(8,128)(2,1)S(1)}, bf16[2048,16,1]{1,0,2:T(8,128)(2,1)}, u32[]{:S(2)}) copy-start(bf16[2048,16,1]{1,0,2:T(8,128)(2,1)} %get-tuple-element.197) | copy-start | bytes 196612
  159.5 9.8 %copy-start.10 = (bf16[2048,16,1]{1,0,2:T(8,128)(2,1)S(1)}, bf16[2048,16,1]{1,0,2:T(8,128)(2,1)}, u32[]{:S(2)}) copy-start(bf16[2048,16,1]{1,0,2:T(8,128)(2,1)} %get-tuple-element.198) | copy-start | bytes 196612
  169.3 10.2 %copy-start.9 = (bf16[2048,16,1]{1,0,2:T(8,128)(2,1)S(1)}, bf16[2048,16,1]{1,0,2:T(8,128)(2,1)}, u32[]{:S(2)}) copy-start(bf16[2048,16,1]{1,0,2:T(8,128)(2,1)} %get-tuple-element.193) | copy-start | bytes 196612
  179.5 9.8 %copy-start.2 = (bf16[2048,128]{1,0:T(8,128)(2,1)S(1)}, bf16[2048,128]{1,0:T(8,128)(2,1)}, u32[]{:S(2)}) copy-start(bf16[2048,128]{1,0:T(8,128)(2,1)} %param.8) | copy-start | bytes 1572868
  194.2 16.9 %all-to-all-start = ((bf16[8,2,16384]{2,1,0:T(2,128)(2,1)}), bf16[8,2,16384]{2,1,0:T(2,128)(2,1)}, u32[]{:S(2)}, u32[]{:S(2)}) async-start(bf16[8,2,16384]{2,1,0:T(2,128)(2,1)} %reshape.197), calls=%async_computation | async-start | bytes 1048576 | tf_op jit(solution)/shard_map/all_to_all | solution.py:108
  263.8 7.8 %collective-permute-start.1 = (bf16[256,1,255]{2,1,0:T(2,128)(2,1)S(1)}, bf16[256,1,255]{2,1,0:T(2,128)(2,1)S(1)}, u32[]{:S(2)}, u32[]{:S(2)}) collective-permute-start(bf16[256,1,255]{2,1,0:T(2,128)(2,1)S(1)} %get-tuple-element.147), channel_id=1, source_target_pairs={{0,2},{2,4},{4,6},{6,8},{8,10},{10,12},{12,14},{14,0},{1,3},{3,5},... | collective-permute-start | bytes 391688 | tf_op jit(solution)/shard_map/ppermute | solution.py:26
  265.5 12.0 %collective-permute-start.2 = (bf16[256,1,255]{2,1,0:T(2,128)(2,1)S(1)}, bf16[256,1,255]{2,1,0:T(2,128)(2,1)S(1)}, u32[]{:S(2)}, u32[]{:S(2)}) collective-permute-start(bf16[256,1,255]{2,1,0:T(2,128)(2,1)S(1)} %get-tuple-element.146), channel_id=1, source_target_pairs={{0,4},{2,6},{4,8},{6,10},{8,12},{10,14},{12,0},{14,2},{1,5},{3,7},... | collective-permute-start | bytes 391688 | tf_op jit(solution)/shard_map/ppermute | solution.py:26
  267.5 37.2 %collective-permute-start.3 = (bf16[256,1,255]{2,1,0:T(2,128)(2,1)S(1)}, bf16[256,1,255]{2,1,0:T(2,128)(2,1)S(1)}, u32[]{:S(2)}, u32[]{:S(2)}) collective-permute-start(bf16[256,1,255]{2,1,0:T(2,128)(2,1)S(1)} %get-tuple-element.145), channel_id=1, source_target_pairs={{0,6},{2,8},{4,10},{6,12},{8,14},{10,0},{12,2},{14,4},{1,7},{3,9},... | collective-permute-start | bytes 391688 | tf_op jit(solution)/shard_map/ppermute | solution.py:26
  269.9 40.5 %collective-permute-start.4 = (bf16[256,1,255]{2,1,0:T(2,128)(2,1)S(1)}, bf16[256,1,255]{2,1,0:T(2,128)(2,1)S(1)}, u32[]{:S(2)}, u32[]{:S(2)}) collective-permute-start(bf16[256,1,255]{2,1,0:T(2,128)(2,1)S(1)} %get-tuple-element.144), channel_id=1, source_target_pairs={{0,8},{2,10},{4,12},{6,14},{8,0},{10,2},{12,4},{14,6},{1,9},{3,11}... | collective-permute-start | bytes 391688 | tf_op jit(solution)/shard_map/ppermute | solution.py:26
  269.9 40.5 %collective-permute-start.5 = (bf16[256,1,255]{2,1,0:T(2,128)(2,1)S(1)}, bf16[256,1,255]{2,1,0:T(2,128)(2,1)S(1)}, u32[]{:S(2)}, u32[]{:S(2)}) collective-permute-start(bf16[256,1,255]{2,1,0:T(2,128)(2,1)S(1)} %get-tuple-element.143), channel_id=1, source_target_pairs={{0,10},{2,12},{4,14},{6,0},{8,2},{10,4},{12,6},{14,8},{1,11},{3,13... | collective-permute-start | bytes 391688 | tf_op jit(solution)/shard_map/ppermute | solution.py:26
  271.6 43.8 %collective-permute-start.6 = (bf16[256,1,255]{2,1,0:T(2,128)(2,1)S(1)}, bf16[256,1,255]{2,1,0:T(2,128)(2,1)S(1)}, u32[]{:S(2)}, u32[]{:S(2)}) collective-permute-start(bf16[256,1,255]{2,1,0:T(2,128)(2,1)S(1)} %get-tuple-element.142), channel_id=1, source_target_pairs={{0,12},{2,14},{4,0},{6,2},{8,4},{10,6},{12,8},{14,10},{1,13},{3,15... | collective-permute-start | bytes 391688 | tf_op jit(solution)/shard_map/ppermute | solution.py:26
  277.5 37.9 %collective-permute-start.7 = (bf16[256,1,255]{2,1,0:T(2,128)(2,1)S(1)}, bf16[256,1,255]{2,1,0:T(2,128)(2,1)S(1)}, u32[]{:S(2)}, u32[]{:S(2)}) collective-permute-start(bf16[256,1,255]{2,1,0:T(2,128)(2,1)S(1)} %get-tuple-element.141), channel_id=1, source_target_pairs={{0,14},{2,0},{4,2},{6,4},{8,6},{10,8},{12,10},{14,12},{1,15},{3,1}... | collective-permute-start | bytes 391688 | tf_op jit(solution)/shard_map/ppermute | solution.py:26
  358.1 14.2 %copy-start.8 = (bf16[2048,16,1]{1,0,2:T(8,128)(2,1)S(1)}, bf16[2048,16,1]{1,0,2:T(8,128)(2,1)}, u32[]{:S(2)}) copy-start(bf16[2048,16,1]{1,0,2:T(8,128)(2,1)} %get-tuple-element.190) | copy-start | bytes 196612
  364.0 17.2 %copy-start.7 = (bf16[2048,16,1]{1,0,2:T(8,128)(2,1)S(1)}, bf16[2048,16,1]{1,0,2:T(8,128)(2,1)}, u32[]{:S(2)}) copy-start(bf16[2048,16,1]{1,0,2:T(8,128)(2,1)} %get-tuple-element.185) | copy-start | bytes 196612
  399.2 8.8 %copy-start.5 = (bf16[2048,16,1]{1,0,2:T(8,128)(2,1)S(1)}, bf16[2048,16,1]{1,0,2:T(8,128)(2,1)}, u32[]{:S(2)}) copy-start(bf16[2048,16,1]{1,0,2:T(8,128)(2,1)} %get-tuple-element.187) | copy-start | bytes 196612
  417.7 10.0 %copy-start.4 = (bf16[2048,16,1]{1,0,2:T(8,128)(2,1)S(1)}, bf16[2048,16,1]{1,0,2:T(8,128)(2,1)}, u32[]{:S(2)}) copy-start(bf16[2048,16,1]{1,0,2:T(8,128)(2,1)} %get-tuple-element.192) | copy-start | bytes 196612
  437.4 10.0 %copy-start.3 = (bf16[2048,128]{1,0:T(8,128)(2,1)S(1)}, bf16[2048,128]{1,0:T(8,128)(2,1)}, u32[]{:S(2)}) copy-start(bf16[2048,128]{1,0:T(8,128)(2,1)} %param.13) | copy-start | bytes 1572868
  (9 other events, 56.0 us)
